TPU v7x, 32 devices: a whole 2x2x4 slice. The times are simulated.
32 devices in a mesh: ctx: 8 (over z, x), chan: 4 (over y, core).
Axes of the slice: x: 2, y: 2, z: 4, core: 2. Of those that a mesh axis runs over, the one named last changes fastest.
Arguments:
- query_in: bfloat16 [4096, 1024], P('chan', 'ctx'), may hold values from -6 to 6
- key_in: bfloat16 [4096, 1024], P('chan', 'ctx'), may hold values from -6 to 6
- value_in: bfloat16 [4096, 1024], P('chan', 'ctx'), may hold values from -6 to 6
- short_kernel: float32 [3, 3, 4096], P(None, None, 'chan'), may hold values from -3.5 to 3.5
- filter_in: float32 [64, 64], replicated, may hold values from -0.75 to 0.75
- filter_out: float32 [64, 4096], P(None, 'chan'), may hold values from -0.75 to 0.75
- filter_decay: float32 [4096], P('chan'), may hold values from 0.5 to 40
- skip_gain: float32 [4096], P('chan'), may hold values from -3 to 3
- grad_out: bfloat16 [4096, 1024], P('chan', 'ctx'), may hold values from -6 to 6
Outputs:
- output: bfloat16 [4096, 1024], P('chan', 'ctx')
- grad_query: bfloat16 [4096, 1024], P('chan', 'ctx')
- grad_key: bfloat16 [4096, 1024], P('chan', 'ctx')
- grad_value: bfloat16 [4096, 1024], P('chan', 'ctx')
- grad_short: float32 [3, 3, 4096], P(None, None, 'chan')
- grad_filter_in: float32 [64, 64], replicated
- grad_filter_out: float32 [64, 4096], P(None, 'chan')
- grad_decay: float32 [4096], P('chan')
- grad_skip: float32 [4096], P('chan')
All inputs are finite; a program needn't handle non-finite values.
Results may differ from a plain program's by a relative error of at most 0.0006.
Values may be sent and summed in bfloat16 or wider, within the bound.
No kernel may reach another device: no remote copies, remote signals or barrier semaphores. Data moves between devices by JAX's collectives and lax.ppermute only.
A program may use at most 128 MiB of HBM per device.

v0:
```python
import math

import jax
import jax.numpy as jnp
from jax import lax
from jax.sharding import PartitionSpec as P

PRECISE = lax.Precision.HIGHEST


def shifted(value, axis, by):
    peers = lax.axis_size(axis)
    pairs = [(i, i + by) for i in range(peers) if 0 <= i + by < peers]
    return lax.ppermute(value, axis, pairs)


def position_features(position, sequence, feature_rows):
    bands = jnp.arange(feature_rows // 2, dtype=jnp.int32)
    factor = 4 * (bands + 1) * (bands + 1)
    phase = position[None, :] * factor[:, None] % sequence
    angles = 2.0 * math.pi / sequence * phase.astype(jnp.float32)
    return jnp.concatenate([jnp.cos(angles), jnp.sin(angles)], axis=0)


def angle_tables(left_index, right_index, modulus):
    phase = left_index[:, None] * right_index[None, :] % modulus
    angles = 2.0 * math.pi / modulus * phase.astype(jnp.float32)
    return (jnp.cos(angles), jnp.sin(angles))


def contract(form, left, right):
    return jnp.einsum(form, left, right, precision=PRECISE)


def times_forward(real_part, imag_part, cosine, sine):
    return (real_part * cosine + imag_part * sine, imag_part * cosine - real_part * sine)


def times_inverse(real_part, imag_part, cosine, sine):
    return (real_part * cosine - imag_part * sine, imag_part * cosine + real_part * sine)


def complex_times(first_real, first_imag, second_real, second_imag):
    return (
        first_real * second_real - first_imag * second_imag,
        first_real * second_imag + first_imag * second_real,
    )


def local_forward(real_part, imag_part):
    length = real_part.shape[-1]
    inner = 64
    outer = length // inner
    leading = real_part.shape[:-1]
    real_part = real_part.reshape(leading + (outer, inner))
    imag_part = imag_part.reshape(leading + (outer, inner))
    outer_index = jnp.arange(outer, dtype=jnp.int32)
    inner_index = jnp.arange(inner, dtype=jnp.int32)
    cos_outer, sin_outer = angle_tables(outer_index, outer_index, outer)
    first_real = contract("cb,...ba->...ca", cos_outer, real_part) + contract(
        "cb,...ba->...ca", sin_outer, imag_part
    )
    first_imag = contract("cb,...ba->...ca", cos_outer, imag_part) - contract(
        "cb,...ba->...ca", sin_outer, real_part
    )
    cos_middle, sin_middle = angle_tables(outer_index, inner_index, length)
    first_real, first_imag = times_forward(first_real, first_imag, cos_middle, sin_middle)
    cos_inner, sin_inner = angle_tables(inner_index, inner_index, inner)
    final_real = contract("...ca,da->...cd", first_real, cos_inner) + contract(
        "...ca,da->...cd", first_imag, sin_inner
    )
    final_imag = contract("...ca,da->...cd", first_imag, cos_inner) - contract(
        "...ca,da->...cd", first_real, sin_inner
    )
    return (final_real, final_imag)


def local_inverse(real_part, imag_part):
    outer = real_part.shape[-2]
    inner = real_part.shape[-1]
    length = outer * inner
    leading = real_part.shape[:-2]
    outer_index = jnp.arange(outer, dtype=jnp.int32)
    inner_index = jnp.arange(inner, dtype=jnp.int32)
    cos_inner, sin_inner = angle_tables(inner_index, inner_index, inner)
    first_real = contract("...cd,ad->...ca", real_part, cos_inner) - contract(
        "...cd,ad->...ca", imag_part, sin_inner
    )
    first_imag = contract("...cd,ad->...ca", imag_part, cos_inner) + contract(
        "...cd,ad->...ca", real_part, sin_inner
    )
    cos_middle, sin_middle = angle_tables(outer_index, inner_index, length)
    first_real, first_imag = times_inverse(first_real, first_imag, cos_middle, sin_middle)
    cos_outer, sin_outer = angle_tables(outer_index, outer_index, outer)
    final_real = contract("bc,...ca->...ba", cos_outer, first_real) - contract(
        "bc,...ca->...ba", sin_outer, first_imag
    )
    final_imag = contract("bc,...ca->...ba", cos_outer, first_imag) + contract(
        "bc,...ca->...ba", sin_outer, first_real
    )
    return (final_real.reshape(leading + (length,)), final_imag.reshape(leading + (length,)))


def held_frequencies(device):
    return 2 * device + jnp.arange(2, dtype=jnp.int32)


def forward_spectrum(signals):
    shards = lax.axis_size("ctx")
    device = lax.axis_index("ctx")
    signal_count, channels, length = signals.shape
    padded = 2 * shards * length
    columns = lax.all_to_all(
        signals.reshape((1, signal_count, channels, length)),
        "ctx",
        split_axis=3,
        concat_axis=0,
        tiled=True,
    )
    shard_index = jnp.arange(shards, dtype=jnp.int32)
    freq_index = jnp.arange(2 * shards, dtype=jnp.int32)
    cos_table, sin_table = angle_tables(freq_index, shard_index, 2 * shards)
    rows_real = contract("qp,pmgb->qmgb", cos_table, columns)
    rows_imag = -contract("qp,pmgb->qmgb", sin_table, columns)
    arrived = lax.all_to_all(
        jnp.stack([rows_real, rows_imag]), "ctx", split_axis=1, concat_axis=4, tiled=True
    )
    spec_real = arrived[0]
    spec_imag = arrived[1]
    freqs = held_frequencies(device)
    cosine, sine = angle_tables(freqs, jnp.arange(length, dtype=jnp.int32), padded)
    spec_real, spec_imag = times_forward(
        spec_real, spec_imag, cosine[:, None, None, :], sine[:, None, None, :]
    )
    return local_forward(spec_real, spec_imag)


def inverse_columns(spec_real, spec_imag):
    shards = lax.axis_size("ctx")
    device = lax.axis_index("ctx")
    real_part, imag_part = local_inverse(spec_real, spec_imag)
    length = real_part.shape[-1]
    padded = 2 * shards * length
    freqs = held_frequencies(device)
    cosine, sine = angle_tables(freqs, jnp.arange(length, dtype=jnp.int32), padded)
    real_part, imag_part = times_inverse(
        real_part, imag_part, cosine[:, None, None, :], sine[:, None, None, :]
    )
    shard_index = jnp.arange(shards, dtype=jnp.int32)
    arrived = lax.all_to_all(
        jnp.stack([real_part, imag_part]), "ctx", split_axis=4, concat_axis=1, tiled=True
    )
    cos_table, sin_table = angle_tables(
        shard_index, jnp.arange(2 * shards, dtype=jnp.int32), 2 * shards
    )
    columns = contract("pq,qmgb->pmgb", cos_table, arrived[0]) - contract(
        "pq,qmgb->pmgb", sin_table, arrived[1]
    )
    return columns * (1.0 / padded)


def to_tokens(columns):
    arrived = lax.all_to_all(columns, "ctx", split_axis=0, concat_axis=3, tiled=True)
    return arrived[0]


def body(
    query_in,
    key_in,
    value_in,
    short_kernel,
    filter_in,
    filter_out,
    filter_decay,
    skip_gain,
    grad_out,
):
    shards = lax.axis_size("ctx")
    device = lax.axis_index("ctx")
    length = query_in.shape[1]
    sequence = shards * length
    scale = sequence ** (-0.5)
    inputs = jnp.stack([query_in, key_in, value_in])
    rim = shifted(inputs[:, :, -2:], "ctx", 1)
    values = inputs.astype(jnp.float32)
    rim_values = rim.astype(jnp.float32)
    before_one = jnp.concatenate([rim_values[..., 1:], values[..., :-1]], axis=-1)
    before_two = jnp.concatenate([rim_values, values[..., :-2]], axis=-1)
    kernel = short_kernel[:, :, :, None]
    shorted = kernel[:, 0] * values + kernel[:, 1] * before_one + kernel[:, 2] * before_two
    query_short = shorted[0]
    key_short = shorted[1]
    value_short = shorted[2]
    gate = key_short * value_short
    position = device * length + jnp.arange(length, dtype=jnp.int32)
    fraction = position.astype(jnp.float32) / sequence
    basis = position_features(position, sequence, filter_in.shape[0])
    preact = jnp.dot(filter_in.T, basis, precision=PRECISE)
    hidden = jnp.sin(preact)
    window = jnp.exp(-filter_decay[:, None] * fraction[None, :])
    taps = window * jnp.dot(filter_out.T, hidden, precision=PRECISE) * scale
    spec_real, spec_imag = forward_spectrum(jnp.stack([gate, taps]))
    gate_real, gate_imag = (spec_real[:, 0], spec_imag[:, 0])
    taps_real, taps_imag = (spec_real[:, 1], spec_imag[:, 1])
    prod_real, prod_imag = complex_times(gate_real, gate_imag, taps_real, taps_imag)
    conv = to_tokens(inverse_columns(prod_real[:, None], prod_imag[:, None]))[0]
    mixed = conv + skip_gain[:, None] * gate
    output = (query_short * mixed).astype(jnp.bfloat16)
    upstream = grad_out.astype(jnp.float32)
    grad_mixed = upstream * query_short
    grad_query_short = upstream * mixed
    upper_real, upper_imag = forward_spectrum(grad_mixed[None])
    upper_real = upper_real[:, 0]
    upper_imag = upper_imag[:, 0]
    along_real, along_imag = complex_times(taps_real, -taps_imag, upper_real, upper_imag)
    cross_real, cross_imag = complex_times(gate_real, -gate_imag, upper_real, upper_imag)
    backward = to_tokens(
        inverse_columns(
            jnp.stack([along_real, cross_real], axis=1), jnp.stack([along_imag, cross_imag], axis=1)
        )
    )
    grad_gate = backward[0] + skip_gain[:, None] * grad_mixed
    grad_taps = backward[1]
    grads = jnp.stack([grad_query_short, grad_gate * value_short, grad_gate * key_short])
    after = shifted(grads[..., :2], "ctx", -1)
    next_one = jnp.concatenate([grads[..., 1:], after[..., :1]], axis=-1)
    next_two = jnp.concatenate([grads[..., 2:], after], axis=-1)
    grad_inputs = (kernel[:, 0] * grads + kernel[:, 1] * next_one + kernel[:, 2] * next_two).astype(
        jnp.bfloat16
    )
    short_terms = jnp.stack(
        [
            jnp.sum(grads * values, axis=-1),
            jnp.sum(grads * before_one, axis=-1),
            jnp.sum(grads * before_two, axis=-1),
        ],
        axis=1,
    )
    weighted = grad_taps * window * scale
    out_terms = jnp.dot(hidden, weighted.T, precision=PRECISE)
    grad_hidden = jnp.dot(filter_out, weighted, precision=PRECISE)
    in_terms = jnp.dot(basis, (grad_hidden * jnp.cos(preact)).T, precision=PRECISE)
    decay_terms = jnp.sum(grad_taps * taps * -fraction[None, :], axis=1)
    skip_terms = jnp.sum(grad_mixed * gate, axis=1)
    short_sum, out_sum, decay_sum, skip_sum = lax.psum(
        (short_terms, out_terms, decay_terms, skip_terms), "ctx"
    )
    in_sum = lax.psum(in_terms, ("ctx", "chan"))
    return (
        output,
        grad_inputs[0],
        grad_inputs[1],
        grad_inputs[2],
        short_sum * scale,
        in_sum * scale,
        out_sum * scale,
        decay_sum * scale,
        skip_sum * scale,
    )


def solution(mesh):
    placed = (
        P("chan", "ctx"),
        P("chan", "ctx"),
        P("chan", "ctx"),
        P(None, None, "chan"),
        P(),
        P(None, "chan"),
        P("chan"),
        P("chan"),
        P("chan", "ctx"),
    )
    return jax.shard_map(
        body,
        mesh=mesh,
        in_specs=placed,
        out_specs=(
            P("chan", "ctx"),
            P("chan", "ctx"),
            P("chan", "ctx"),
            P("chan", "ctx"),
            P(None, None, "chan"),
            P(),
            P(None, "chan"),
            P("chan"),
            P("chan"),
        ),
        check_vma=False,
    )
```

profile of v0, /device:TPU:0, one launch (start us, length us, event | category | flops | bytes accessed | tf_op | source)
XLA Modules:
  0.0 650.8 jit_solution(13803028707653949594)
XLA Ops:
  11.0 4.8 collective-permute-start
  20.5 6.6 %all-to-all-start.4 = ((f32[1,1,1024,128]{2,1,0,3:T(1,128)}), f32[1,1,1024,128]{2,1,0,3:T(1,128)}, u32[]{:S(2)}, u32[]{:S(2)}) async-start(f32[1,1,1024,128]{2,1,0,3:T(1,128)} %copy.246), calls=%async_computation.4 | async-start | bytes 1048576 | tf_op jit(solution)/shard_map/all_to_all | solution.py:113
  32.8 7.8 %all-to-all-done.4 = f32[1,1,1024,128]{2,1,0,3:T(1,128)} async-done(((f32[1,1,1024,128]{2,1,0,3:T(1,128)}), f32[1,1,1024,128]{2,1,0,3:T(1,128)}, u32[]{:S(2)}, u32[]{:S(2)}) %all-to-all-start.4) | async-done | bytes 524320 | tf_op jit(solution)/shard_map/all_to_all | solution.py:113
  40.6 4.2 all-to-all-start
  48.6 2.6 copy.248
  51.2 18.4 %all-to-all-done = f32[1,2,1024,128]{2,1,0,3:T(2,128)} async-done(((f32[1,2,1024,128]{2,1,0,3:T(2,128)}), f32[1,2,1024,128]{2,1,0,3:T(2,128)}, u32[]{:S(2)}, u32[]{:S(2)}) %all-to-all-start) | async-done | bytes 1048608 | tf_op jit(solution)/shard_map/all_to_all | solution.py:113
  69.6 4.6 all-to-all-start.5
  74.2 3.4 negate_bitcast_fusion
  77.6 3.4 convolution_bitcast_fusion
  81.6 4.4 copy.220
  86.1 35.7 %all-to-all-done.5 = f32[2,16,1,1024,16]{3,4,2,0,1:T(8,128)} async-done(((f32[2,16,1,1024,16]{3,4,2,0,1:T(8,128)}), f32[2,16,1,1024,16]{3,4,2,0,1:T(8,128)}, u32[]{:S(2)}, u32[]{:S(2)}) %all-to-all-start.5) | async-done | bytes 2097184 | tf_op jit(solution)/shard_map/all_to_all | solution.py:125
  121.8 5.0 all-to-all-start.1
  132.8 4.1 fusion.61
  136.9 4.3 fusion.35
  141.2 4.1 fusion.65
  145.3 5.7 subtract_bitcast_fusion.1
  152.5 2.5 fusion.34
  155.0 2.4 fusion.55
  157.5 61.8 %all-to-all-done.1 = f32[2,16,2,1024,16]{3,4,2,0,1:T(8,128)} async-done(((f32[2,16,2,1024,16]{3,4,2,0,1:T(8,128)}), f32[2,16,2,1024,16]{3,4,2,0,1:T(8,128)}, u32[]{:S(2)}, u32[]{:S(2)}) %all-to-all-start.1) | async-done | bytes 4194336 | tf_op jit(solution)/shard_map/all_to_all | solution.py:125
  219.3 2.5 copy.221
  224.1 7.9 %fusion.26 = f32[2,2,1024,64,2]{2,4,3,1,0:T(2,128)S(1)} fusion(f32[2,2,1024,2,64]{2,4,3,1,0:T(8,128)S(1)} %get-tuple-element.68), kind=kOutput, calls=%fused_computation.48 | convolution fusion | flops 12582968 | bytes 4194304 | tf_op jit(solution)/shard_map/cb,...ba->...ca/dot_general | solution.py:32
  232.0 8.1 %fusion.22 = f32[2,2,1024,64,2]{2,4,3,1,0:T(2,128)S(1)} fusion(f32[2,2,1024,2,64]{2,4,3,1,0:T(8,128)S(1)} %get-tuple-element.69), kind=kOutput, calls=%fused_computation.44 | convolution fusion | flops 12582968 | bytes 4194304 | tf_op jit(solution)/shard_map/cb,...ba->...ca/dot_general | solution.py:32
  240.1 8.2 %convolution_add_fusion = f32[2,2,1024,64,2]{2,4,3,1,0:T(2,128)S(1)} fusion(f32[2,2,1024,64,2]{2,4,3,1,0:T(2,128)S(1)} %fusion.26, f32[2,2,1024,2,64]{2,4,3,1,0:T(8,128)S(1)} %get-tuple-element.69), kind=kOutput, calls=%fused_computation.42 | convolution fusion | flops 13107256 | bytes 6291456 | tf_op jit(solution)/shard_map/cb,...ba->...ca/dot_general | solution.py:32
  248.3 11.4 %fusion.2 = (f32[2,2,1024,2,64]{2,3,4,1,0:T(2,128)S(1)}, f32[2,2,1024,2,64]{2,3,4,1,0:T(2,128)S(1)}) fusion(f32[2,2,1024,64,2]{2,4,3,1,0:T(2,128)S(1)} %convolution_add_fusion, f32[2,64]{0,1:T(8,128)S(1)} %copy-done.21, f32[2,64]{0,1:T(8,128)S(1)} %copy-done.23, f32[2,2,1024,64,2]{2,4,3,1,0:T(2,128)S(1)} %fusion.22, ...), kind=kOutput, calls=%fused_computation.14 | convolution fusion | flops 16252984 | bytes 10486784 | tf_op jit(solution)/shard_map/cb,...ba->...ca/dot_general | solution.py:32
  259.7 2.8 fusion.4
  262.6 2.8 fusion.6
  265.4 3.1 fusion.16
  268.6 3.1 fusion.19
  271.7 3.8 multiply_subtract_fusion.3
  277.8 2.4 fusion.15
  284.8 9.4 %multiply_subtract_fusion = (f32[2,2,1024,2,64]{2,3,4,1,0:T(2,128)S(1)}, f32[2,2,1024,2,64]{2,3,4,1,0:T(2,128)S(1)}) fusion(f32[2,64]{0,1:T(8,128)S(1)} %copy-done.21, f32[2,64]{0,1:T(8,128)S(1)} %copy-done.23, f32[2,2,1024,2,64]{2,4,3,1,0:T(8,128)S(1)} %fusion.13, f32[2,2,1024,2,64]{2,4,3,1,0:T(8,128)S(1)} %fusion.15, ...), kind=kLoop, calls=%fused_computation.23 | loop fusion | flops 4194304 | bytes 12583936 | tf_op jit(solution)/shard_map/sub | solution.py:40
  294.3 7.5 %fusion.190 = f32[2,2,1024,64,2]{2,4,3,1,0:T(2,128)S(1)} fusion(f32[2,2,1024,2,64]{2,3,4,1,0:T(2,128)S(1)} %get-tuple-element.60), kind=kOutput, calls=%fused_computation.283 | convolution fusion | flops 12582968 | bytes 4194304 | tf_op jit(solution)/shard_map/bc,...ca->...ba/dot_general | solution.py:32
  301.8 7.5 %fusion.188 = f32[2,2,1024,64,2]{2,4,3,1,0:T(2,128)S(1)} fusion(f32[2,2,1024,2,64]{2,3,4,1,0:T(2,128)S(1)} %get-tuple-element.61), kind=kOutput, calls=%fused_computation.281 | convolution fusion | flops 12582968 | bytes 4194304 | tf_op jit(solution)/shard_map/bc,...ca->...ba/dot_general | solution.py:32
  309.3 8.6 %subtract_bitcast_fusion = f32[2,2,1024,2,64]{2,3,4,1,0:T(2,128)S(1)} fusion(f32[2,2,1024,64,2]{2,4,3,1,0:T(2,128)S(1)} %fusion.190, f32[2,2,1024,2,64]{2,3,4,1,0:T(2,128)S(1)} %get-tuple-element.61), kind=kOutput, calls=%fused_computation.21 | convolution fusion | flops 13107256 | bytes 6291456 | tf_op jit(solution)/shard_map/bc,...ca->...ba/dot_general | solution.py:32
  318.0 8.0 %add_bitcast_fusion = f32[2,2,1024,2,64]{2,3,4,1,0:T(2,128)S(1)} fusion(f32[2,2,1024,64,2]{2,4,3,1,0:T(2,128)S(1)} %fusion.188, f32[2,2,1024,2,64]{2,3,4,1,0:T(2,128)S(1)} %get-tuple-element.60), kind=kOutput, calls=%fused_computation.20 | convolution fusion | flops 13107256 | bytes 6291456 | tf_op jit(solution)/shard_map/bc,...ca->...ba/dot_general | solution.py:32
  328.9 5.2 copy.268
  334.1 4.7 all-to-all-start.6
  338.9 2.6 fusion.45
  345.6 4.1 fusion.67
  349.7 4.3 fusion.37
  354.3 4.1 fusion.71
  358.4 4.6 fusion.38
  363.9 2.9 copy.240
  366.9 64.5 %all-to-all-done.6 = f32[2,2,2,1024,128]{3,2,1,0,4:T(2,128)} async-done(((f32[2,2,2,1024,128]{3,2,1,0,4:T(2,128)}), f32[2,2,2,1024,128]{3,2,1,0,4:T(2,128)}, u32[]{:S(2)}, u32[]{:S(2)}) %all-to-all-start.6) | async-done | bytes 4194336 | tf_op jit(solution)/shard_map/all_to_all | solution.py:150
  431.4 4.4 all-to-all-start.2
  435.8 4.6 copy.269
  442.2 3.0 copy.271
  445.2 3.7 squeeze.65
  448.9 4.6 copy.270
  453.5 3.7 squeeze.64
  457.2 2.9 fusion.137
  462.8 20.8 %all-to-all-done.2 = f32[2,2,1,1024,128]{3,1,2,0,4:T(2,128)} async-done(((f32[2,2,1,1024,128]{3,1,2,0,4:T(2,128)}), f32[2,2,1,1024,128]{3,1,2,0,4:T(2,128)}, u32[]{:S(2)}, u32[]{:S(2)}) %all-to-all-start.2) | async-done | bytes 2097184 | tf_op jit(solution)/shard_map/all_to_all | solution.py:150
  483.6 4.4 all-to-all-start.7
  488.0 2.8 copy.241
  493.7 2.9 reshape.382
  496.7 3.0 copy.242
  499.7 2.9 reshape.381
  506.3 7.3 %all-to-all-done.7 = f32[8,2,1024,16]{2,3,1,0:T(8,128)} async-done(((f32[8,2,1024,16]{2,3,1,0:T(8,128)}), f32[8,2,1024,16]{2,3,1,0:T(8,128)}, u32[]{:S(2)}, u32[]{:S(2)}) %all-to-all-start.7) | async-done | bytes 1048608 | tf_op jit(solution)/shard_map/all_to_all | solution.py:163
  513.6 4.1 all-to-all-start.3
  523.2 40.9 %psum.36 = f32[64,64]{1,0:T(8,128)S(1)} all-reduce(f32[64,64]{1,0:T(8,128)} %fusion.105), channel_id=1, replica_groups=mesh['ctx'=8,'chan'=4] {'ctx','chan'}, use_global_device_ids=true, to_apply=%region_4.5 | all-reduce | flops 4096 | bytes 32768 | tf_op jit(solution)/shard_map/psum | solution.py:248
  566.9 2.8 fusion.73
  573.9 37.3 %all-reduce = (f32[3,3,1024]{2,0,1:T(4,128)S(1)}, f32[1024]{0:T(1024)S(1)}, f32[1024]{0:T(1024)S(1)}) all-reduce(f32[3,3,1024]{2,0,1:T(4,128)S(1)} %pad_maximum_fusion.14, f32[1024]{0:T(1024)S(1)} %get-tuple-element.106, f32[1024]{0:T(1024)S(1)} %get-tuple-element.96), channel_id=1, replica_groups=mesh['ctx'=8,'chan'=4] {'ctx'}, use_global_device_ids=true, to_apply=%region_3.4 | all-reduce | flops 11264 | bytes 90112 | tf_op jit(solution)/shard_map/psum | solution.py:245
  614.8 2.7 collective-permute-done.1
  620.8 21.3 %all-reduce.3.cloned.1.call-done = f32[64,1024]{1,0:T(8,128)} async-done(((f32[64,1024]{1,0:T(8,128)}), f32[64,1024]{1,0:T(8,128)}) %all-reduce.3.cloned.1.call-update) | async-done | bytes 262160 | tf_op jit(solution)/shard_map/psum | solution.py:245
  (172 shorter events, 75.1 us)
Async XLA Ops:
  7.2 22.2 %copy-start = (f32[64,1024]{1,0:T(8,128)S(1)}, f32[64,1024]{1,0:T(8,128)}, u32[]{:S(2)}) copy-start(f32[64,1024]{1,0:T(8,128)} %param.14) | copy-start | bytes 786436
  8.3 2.6 copy-start.10
  8.3 7.5 %copy-start.27 = (f32[3,3,1024]{2,1,0:T(4,128)S(1)}, f32[3,3,1024]{2,1,0:T(4,128)}, u32[]{:S(2)}) copy-start(f32[3,3,1024]{2,1,0:T(4,128)} %param.12) | copy-start | bytes 110596
  8.3 7.7 %copy-start.36 = (f32[1024]{0:T(1024)S(1)}, f32[1024]{0:T(1024)}, u32[]{:S(2)}) copy-start(f32[1024]{0:T(1024)} %param.15) | copy-start | bytes 12292
  8.4 7.8 %copy-start.19 = (bf16[1024,128]{1,0:T(8,128)(2,1)S(1)}, bf16[1024,128]{1,0:T(8,128)(2,1)}, u32[]{:S(2)}) copy-start(bf16[1024,128]{1,0:T(8,128)(2,1)} %param.17) | copy-start | bytes 786436
  9.6 7.4 %copy-start.11 = (bf16[1024,128]{0,1:T(8,128)(2,1)}, bf16[1024,128]{0,1:T(8,128)(2,1)S(1)}, u32[]{:S(2)}) copy-start(bf16[1024,128]{0,1:T(8,128)(2,1)S(1)} %copy.215) | copy-start | bytes 786436
  10.8 6.5 copy-start.12
  11.0 6.2 collective-permute-start
  17.3 1.8 copy-start.25
  17.3 1.7 copy-start.18
  20.5 20.0 %all-to-all-start.4 = ((f32[1,1,1024,128]{2,1,0,3:T(1,128)}), f32[1,1,1024,128]{2,1,0,3:T(1,128)}, u32[]{:S(2)}, u32[]{:S(2)}) async-start(f32[1,1,1024,128]{2,1,0,3:T(1,128)} %copy.246), calls=%async_computation.4 | async-start | bytes 1048576 | tf_op jit(solution)/shard_map/all_to_all | solution.py:113
  27.7 1.7 copy-start.37
  30.1 0.8 copy-start.8
  40.6 29.0 %all-to-all-start = ((f32[1,2,1024,128]{2,1,0,3:T(2,128)}), f32[1,2,1024,128]{2,1,0,3:T(2,128)}, u32[]{:S(2)}, u32[]{:S(2)}) async-start(f32[1,2,1024,128]{2,1,0,3:T(2,128)} %copy.217), calls=%async_computation | async-start | bytes 2097152 | tf_op jit(solution)/shard_map/all_to_all | solution.py:113
  69.6 52.2 %all-to-all-start.5 = ((f32[2,16,1,1024,16]{3,4,2,0,1:T(8,128)}), f32[2,16,1,1024,16]{3,4,2,0,1:T(8,128)}, u32[]{:S(2)}, u32[]{:S(2)}) async-start(f32[2,16,1,1024,16]{3,4,2,0,1:T(8,128)} %copy.248), calls=%async_computation.5 | async-start | bytes 4194304 | tf_op jit(solution)/shard_map/all_to_all | solution.py:125
  121.8 97.5 %all-to-all-start.1 = ((f32[2,16,2,1024,16]{3,4,2,0,1:T(8,128)}), f32[2,16,2,1024,16]{3,4,2,0,1:T(8,128)}, u32[]{:S(2)}, u32[]{:S(2)}) async-start(f32[2,16,2,1024,16]{3,4,2,0,1:T(8,128)} %copy.220), calls=%async_computation.1 | async-start | bytes 8388608 | tf_op jit(solution)/shard_map/all_to_all | solution.py:125
  127.4 2.1 copy-start.30
  130.3 2.2 copy-start.28
  141.2 4.1 copy-start.20
  141.2 4.1 copy-start.22
  151.0 4.0 copy-start.15
  222.6 0.7 copy-start.29
  240.1 8.3 %copy-start.21 = (f32[2,64]{0,1:T(8,128)S(1)}, f32[2,64]{0,1:T(8,128)}, u32[]{:S(2)}) copy-start(f32[2,64]{0,1:T(8,128)} %copy.229) | copy-start | bytes 1540
  240.1 8.3 %copy-start.23 = (f32[2,64]{0,1:T(8,128)S(1)}, f32[2,64]{0,1:T(8,128)}, u32[]{:S(2)}) copy-start(f32[2,64]{0,1:T(8,128)} %copy.226) | copy-start | bytes 1540
  268.6 3.1 copy-start.14
  268.6 3.1 copy-start.16
  268.6 3.1 copy-start.17
  326.6 0.7 copy-start.33
  326.6 0.7 copy-start.34
  334.1 97.3 %all-to-all-start.6 = ((f32[2,2,2,1024,128]{3,2,1,0,4:T(2,128)}), f32[2,2,2,1024,128]{3,2,1,0,4:T(2,128)}, u32[]{:S(2)}, u32[]{:S(2)}) async-start(f32[2,2,2,1024,128]{3,2,1,0,4:T(2,128)} %copy.268), calls=%async_computation.6 | async-start | bytes 8388608 | tf_op jit(solution)/shard_map/all_to_all | solution.py:150
  338.9 2.6 copy-start.1
  338.9 3.8 copy-start.2
  342.7 1.3 copy-start.31
  342.7 1.3 copy-start.32
  358.4 4.9 copy-start.35
  431.4 52.2 %all-to-all-start.2 = ((f32[2,2,1,1024,128]{3,1,2,0,4:T(2,128)}), f32[2,2,1,1024,128]{3,1,2,0,4:T(2,128)}, u32[]{:S(2)}, u32[]{:S(2)}) async-start(f32[2,2,1,1024,128]{3,1,2,0,4:T(2,128)} %copy.240), calls=%async_computation.2 | async-start | bytes 4194304 | tf_op jit(solution)/shard_map/all_to_all | solution.py:150
  457.2 2.9 copy-start.3
  483.6 30.0 %all-to-all-start.7 = ((f32[8,2,1024,16]{2,3,1,0:T(8,128)}), f32[8,2,1024,16]{2,3,1,0:T(8,128)}, u32[]{:S(2)}, u32[]{:S(2)}) async-start(f32[8,2,1024,16]{2,3,1,0:T(8,128)} %copy.272), calls=%async_computation.7 | async-start | bytes 2097152 | tf_op jit(solution)/shard_map/all_to_all | solution.py:163
  502.6 2.0 copy-start.13
  513.6 53.3 %all-to-all-start.3 = ((f32[8,1,1024,16]{2,3,1,0:T(8,128)}), f32[8,1,1024,16]{2,3,1,0:T(8,128)}, u32[]{:S(2)}, u32[]{:S(2)}) async-start(f32[8,1,1024,16]{2,3,1,0:T(8,128)} %copy.244), calls=%async_computation.3 | async-start | bytes 1048576 | tf_op jit(solution)/shard_map/all_to_all | solution.py:163
  517.7 124.4 %all-reduce.3.cloned.1.call-start = ((), (), s32[]{:S(2)}) async-start(), calls=%async_computation.8 | async-start | bytes 524288 | tf_op jit(solution)/shard_map/psum | solution.py:245
  517.8 2.2 copy-start.9
  517.8 3.9 copy-start.24
  520.9 0.8 copy-start.7
  566.9 4.7 copy-start.26
  611.8 5.7 collective-permute-start.1
  613.9 3.7 copy-start.4
  613.9 3.7 copy-start.5
  613.9 3.7 copy-start.6
Sparse Core Ops, SparseCore 0:
  571.6 70.4 all-reduce.2
where the time goes:
time: 659 us; the launch traced here: 651 us
  waiting for transfers between devices  240 us (36%)
  matrix products  162 us (25%)
  local copies, waits for them, and re-layouts  82.3 us (12%)
  blocking collectives  78.2 us (12%)
  starting transfers between devices  44.2 us (7%)
  other arithmetic  27.9 us (4%)
  between operations  15.5 us (2%)
    dot_general x40, matrix products, contract(): return jnp.einsum(form, left, right, precision=PRECISE)  156 us
    all_to_all x2, waiting for transfers between devices, forward_spectrum(): lax.all_to_all(jnp.stack([rows_real, rows_imag]), 'ctx', split_axis=1, co...  97.5 us
    all_to_all x2, waiting for transfers between devices, inverse_columns(): lax.all_to_all(jnp.stack([real_part, imag_part]), 'ctx', split_axis=4, co...  85.3 us
    psum x1, blocking collectives, body(): in_sum = lax.psum(in_terms, ('ctx', 'chan'))  40.9 us
    psum x1, blocking collectives, body(): lax.psum((short_terms, out_terms, decay_terms, skip_terms), 'ctx')  37.3 us
    all_to_all x2, waiting for transfers between devices, forward_spectrum(): lax.all_to_all(signals.reshape((1, signal_count, channels, length)), 'ctx...  26.2 us
    psum x1, waiting for transfers between devices, body(): lax.psum((short_terms, out_terms, decay_terms, skip_terms), 'ctx')  21.3 us
  transfers between devices with their start and end apart: 11, of which 10 were waited for; matrix products, arithmetic and copies ran while one was open for 22% of the time, Pallas kernels for 0%

commit v1 on v0

--- a/solution.py
+++ b/solution.py
@@ -2,7 +2,10 @@
 
 import jax
 import jax.numpy as jnp
+import numpy as np
 from jax import lax
+from jax.experimental import pallas as pl
+from jax.experimental.pallas import tpu as pltpu
 from jax.sharding import PartitionSpec as P
 
 PRECISE = lax.Precision.HIGHEST
@@ -164,7 +167,7 @@
     return arrived[0]
 
 
-def body(
+def spread_body(
     query_in,
     key_in,
     value_in,
@@ -259,6 +262,369 @@
     )
 
 
+RADIX = 8
+LANES = 128
+ROOT_HALF = math.sqrt(0.5)
+F32 = jnp.float32
+BF16 = jnp.bfloat16
+
+
+def split(value):
+    high = value.astype(BF16)
+    return high, (value - high.astype(F32)).astype(BF16)
+
+
+def host_split(table):
+    high = table.astype(BF16)
+    low = (table - high.astype(np.float64)).astype(BF16)
+    return high, low
+
+
+def host_tables(sequence, feature_rows, length):
+    outer = sequence // RADIX
+    token = RADIX * np.arange(outer)[None, :] + np.arange(RADIX)[:, None]
+    freq = 4 * np.arange(outer) + 1
+    phase = freq[None, :, None] * token[:, None, :] % (4 * sequence)
+    angle = 2.0 * np.pi * phase / (4 * sequence)
+    forward = np.concatenate([np.cos(angle), -np.sin(angle)], axis=1)
+    high, low = host_split(forward)
+    twice = np.concatenate([high, high], axis=2)
+    inverse = forward.transpose(0, 2, 1) / sequence
+    inverse_high, inverse_low = host_split(inverse)
+    inverse_pair = np.concatenate([inverse_high, inverse_low], axis=1)
+    bands = np.arange(feature_rows // 2)
+    turns = token.reshape(1, -1) * (4 * (bands + 1) ** 2)[:, None] % sequence
+    turn_angle = 2.0 * np.pi * turns / sequence
+    basis = np.concatenate([np.cos(turn_angle), np.sin(turn_angle)], axis=0)
+    group = length // RADIX
+    order = np.zeros((length, length))
+    for r in range(RADIX):
+        for v in range(group):
+            order[r * group + v, RADIX * v + r] = 1.0
+    return (
+        jnp.asarray(twice),
+        jnp.asarray(low),
+        jnp.asarray(inverse_pair),
+        jnp.asarray(basis.astype(np.float32)),
+        jnp.asarray(order.astype(BF16)),
+    )
+
+
+def dot(left, right, left_dim=1, right_dim=0, precision=None):
+    return lax.dot_general(
+        left,
+        right,
+        (((left_dim,), (right_dim,)), ((), ())),
+        precision=precision,
+        preferred_element_type=F32,
+    )
+
+
+def add(a, b):
+    return (a[0] + b[0], a[1] + b[1])
+
+
+def sub(a, b):
+    return (a[0] - b[0], a[1] - b[1])
+
+
+def quarter(a, inverse):
+    return (-a[1], a[0]) if inverse else (a[1], -a[0])
+
+
+def eighth(a, inverse):
+    if inverse:
+        return ((a[0] - a[1]) * ROOT_HALF, (a[0] + a[1]) * ROOT_HALF)
+    return ((a[0] + a[1]) * ROOT_HALF, (a[1] - a[0]) * ROOT_HALF)
+
+
+def four_points(a, b, c, d, inverse):
+    even_sum, even_diff = add(a, c), sub(a, c)
+    odd_sum, odd_diff = add(b, d), quarter(sub(b, d), inverse)
+    return (
+        add(even_sum, odd_sum),
+        add(even_diff, odd_diff),
+        sub(even_sum, odd_sum),
+        sub(even_diff, odd_diff),
+    )
+
+
+def eight_points(x, inverse):
+    even = four_points(x[0], x[2], x[4], x[6], inverse)
+    odd = four_points(x[1], x[3], x[5], x[7], inverse)
+    first = eighth(odd[1], inverse)
+    turned = (odd[0], first, quarter(odd[2], inverse), quarter(eighth(odd[3], inverse), inverse))
+    return [add(e, o) for e, o in zip(even, turned)] + [sub(e, o) for e, o in zip(even, turned)]
+
+
+def times(a, b):
+    return (a[0] * b[0] - a[1] * b[1], a[0] * b[1] + a[1] * b[0])
+
+
+def times_conj(a, b):
+    return (a[0] * b[0] + a[1] * b[1], a[1] * b[0] - a[0] * b[1])
+
+
+def prepare_kernel(
+    fin_ref, fout_ref, decay_ref, basis_ref, twice_ref, low_ref,
+    hidden_ref, slope_ref, window_ref, taps_ref, spec_ref, leaf_ref,
+):
+    outer = window_ref.shape[1]
+    sequence = RADIX * outer
+    scale = sequence ** (-0.5)
+    preact = dot(fin_ref[...], basis_ref[...], 0, 0, PRECISE)
+    hidden = jnp.sin(preact)
+    hidden_ref[...] = hidden
+    slope_ref[...] = jnp.cos(preact)
+    row = lax.broadcasted_iota(jnp.int32, (outer, LANES), 0)
+    for r in range(RADIX):
+        fraction = (RADIX * row + r).astype(F32) / sequence
+        window = jnp.exp(-decay_ref[...] * fraction)
+        window_ref[r] = window
+        mix = dot(hidden[:, r * outer : (r + 1) * outer], fout_ref[...], 0, 0, PRECISE)
+        taps = window * mix * scale
+        taps_ref[r] = taps
+        high, low = split(taps)
+        leaf_ref[r] = dot(twice_ref[r], jnp.concatenate([high, low], axis=0)) + dot(low_ref[r], high)
+    step = 8
+
+    @pl.loop(0, outer // step)
+    def _(chunk):
+        at = pl.multiple_of(chunk * step, step)
+        real = pl.ds(at, step)
+        imag = pl.ds(pl.multiple_of(outer + at, step), step)
+        points = eight_points([(leaf_ref[r, real, :], leaf_ref[r, imag, :]) for r in range(RADIX)], False)
+        for m in range(RADIX):
+            spec_ref[m, real, :] = points[m][0]
+            spec_ref[m, imag, :] = points[m][1]
+
+
+def down(block, first_row):
+    return jnp.where(first_row, 0.0, pltpu.roll(block, 1, 0))
+
+
+def up(block, last_row):
+    return jnp.where(last_row, 0.0, pltpu.roll(block, block.shape[0] - 1, 0))
+
+
+def main_kernel(
+    in_ref, kern_ref, skip_ref, hidden_ref, slope_ref, window_ref, taps_ref, spec_ref,
+    fout_ref, basis_ref, twice_ref, low_ref, pair_ref, order_ref,
+    out_ref, grads_ref, first_ref,
+    tok_ref, gate_ref, mixgrad_ref, short_ref, leaf_ref, qhigh_ref, qlow_ref, short_grad_ref, weighted_ref, done_ref,
+):
+    peers, _, lanes, length = in_ref.shape
+    outer = taps_ref.shape[1]
+    sequence = RADIX * outer
+    group = length // RADIX
+    scale = sequence ** (-0.5)
+    order = order_ref[...]
+    for s in range(peers):
+        for a in range(4):
+            turned = dot(order, in_ref[s, a], 1, 1)
+            for r in range(RADIX):
+                tok_ref[a, r, s * group : (s + 1) * group, :] = turned[r * group : (r + 1) * group]
+    row = lax.broadcasted_iota(jnp.int32, (outer, LANES), 0)
+    first_row = row == 0
+    last_row = row == outer - 1
+    for i in range(3):
+        back = [down(tok_ref[i, RADIX - 2], first_row), down(tok_ref[i, RADIX - 1], first_row)]
+        weights = [kern_ref[3 * i + j : 3 * i + j + 1, :] for j in range(3)]
+        for r in range(RADIX):
+            one = back[1] if r == 0 else tok_ref[i, r - 1]
+            two = back[r] if r < 2 else tok_ref[i, r - 2]
+            short_ref[i, r] = weights[0] * tok_ref[i, r] + weights[1] * one + weights[2] * two
+    for r in range(RADIX):
+        gate = short_ref[1, r] * short_ref[2, r]
+        mixgrad = tok_ref[3, r] * short_ref[0, r]
+        gate_ref[r] = gate
+        mixgrad_ref[r] = mixgrad
+        high, low = split(jnp.concatenate([gate, mixgrad], axis=1))
+        leaf_ref[r] = dot(twice_ref[r], jnp.concatenate([high, low], axis=0)) + dot(low_ref[r], high)
+    step = 16
+
+    @pl.loop(0, outer // step)
+    def _(chunk):
+        at = pl.multiple_of(chunk * step, step)
+        real = pl.ds(at, step)
+        imag = pl.ds(pl.multiple_of(outer + at, step), step)
+        spectra = []
+        for lane in (0, LANES):
+            span = slice(lane, lane + LANES)
+            spectra.append(
+                eight_points(
+                    [(leaf_ref[r, real, span], leaf_ref[r, imag, span]) for r in range(RADIX)], False
+                )
+            )
+        gates, mixes = spectra
+        tap = [(spec_ref[m, real, :], spec_ref[m, imag, :]) for m in range(RADIX)]
+        products = (
+            [times(gates[m], tap[m]) for m in range(RADIX)],
+            [times_conj(mixes[m], tap[m]) for m in range(RADIX)],
+            [times_conj(mixes[m], gates[m]) for m in range(RADIX)],
+        )
+        for n in range(3):
+            span = slice(n * LANES, (n + 1) * LANES)
+            points = eight_points(products[n], True)
+            for r in range(RADIX):
+                for rows, part in ((real, points[r][0]), (imag, points[r][1])):
+                    high, low = split(part)
+                    qhigh_ref[r, rows, span] = high
+                    qlow_ref[r, rows, span] = low
+
+    skip = skip_ref[...]
+    decay_sum = jnp.zeros((1, LANES), F32)
+    skip_sum = jnp.zeros((1, LANES), F32)
+    for r in range(RADIX):
+        both = dot(pair_ref[r], qhigh_ref[r])
+        result = both[:outer] + both[outer:] + dot(pair_ref[r, :outer, :], qlow_ref[r])
+        gate = gate_ref[r]
+        mixgrad = mixgrad_ref[r]
+        mixed = result[:, :LANES] + skip * gate
+        grad_gate = result[:, LANES : 2 * LANES] + skip * mixgrad
+        grad_taps = result[:, 2 * LANES :]
+        done_ref[0, r] = (short_ref[0, r] * mixed).astype(BF16)
+        short_grad_ref[0, r] = tok_ref[3, r] * mixed
+        short_grad_ref[1, r] = grad_gate * short_ref[2, r]
+        short_grad_ref[2, r] = grad_gate * short_ref[1, r]
+        weighted_ref[r * outer : (r + 1) * outer, :] = grad_taps * window_ref[r] * scale
+        fraction = (RADIX * row + r).astype(F32) / sequence
+        decay_sum = decay_sum + jnp.sum(grad_taps * taps_ref[r] * -fraction, axis=0, keepdims=True)
+        skip_sum = skip_sum + jnp.sum(mixgrad * gate, axis=0, keepdims=True)
+    for i in range(3):
+        back = [down(tok_ref[i, RADIX - 2], first_row), down(tok_ref[i, RADIX - 1], first_row)]
+        ahead = [up(short_grad_ref[i, 0], last_row), up(short_grad_ref[i, 1], last_row)]
+        weights = [kern_ref[3 * i + j : 3 * i + j + 1, :] for j in range(3)]
+        sums = [jnp.zeros((1, LANES), F32) for _ in range(3)]
+        for r in range(RADIX):
+            grad = short_grad_ref[i, r]
+            next_one = short_grad_ref[i, r + 1] if r + 1 < RADIX else ahead[0]
+            next_two = short_grad_ref[i, r + 2] if r + 2 < RADIX else ahead[r + 2 - RADIX]
+            done_ref[1 + i, r] = (weights[0] * grad + weights[1] * next_one + weights[2] * next_two).astype(BF16)
+            one = back[1] if r == 0 else tok_ref[i, r - 1]
+            two = back[r] if r < 2 else tok_ref[i, r - 2]
+            for j, value in enumerate((tok_ref[i, r], one, two)):
+                sums[j] = sums[j] + jnp.sum(grad * value, axis=0, keepdims=True)
+        for j in range(3):
+            grads_ref[3 * i + j : 3 * i + j + 1, :] = sums[j] * scale
+    grads_ref[9:10, :] = decay_sum * scale
+    grads_ref[10:11, :] = skip_sum * scale
+    grads_ref[11:16, :] = jnp.zeros((5, LANES), F32)
+    weighted = weighted_ref[...]
+    grads_ref[16:, :] = dot(hidden_ref[...], weighted, 1, 0, PRECISE) * scale
+    grad_hidden = dot(fout_ref[...], weighted, 1, 1, PRECISE)
+    first_ref[...] = dot(basis_ref[...], grad_hidden * slope_ref[...], 1, 1, PRECISE) * scale
+    for s in range(peers):
+        for a in range(4):
+            rows = jnp.concatenate(
+                [done_ref[a, r, s * group : (s + 1) * group, :] for r in range(RADIX)], axis=0
+            )
+            out_ref[s, a] = dot(rows, order, 0, 0).astype(BF16)
+
+
+def exchange(value, axis, by):
+    return lax.ppermute(value, axis, [(i, i ^ by) for i in range(lax.axis_size(axis))])
+
+
+def blocks_body(
+    query_in, key_in, value_in, short_kernel, filter_in, filter_out, filter_decay, skip_gain, grad_out
+):
+    shards = lax.axis_size("ctx")
+    groups = lax.axis_size("chan")
+    device = lax.axis_index("ctx")
+    channels, length = query_in.shape
+    sequence = shards * length
+    outer = sequence // RADIX
+    mine = channels // shards
+    order = filter_out.shape[0]
+    features = filter_in.shape[0]
+    twice, low, pair, basis, turn = host_tables(sequence, features, length)
+    sent = jnp.stack(
+        [a.reshape(shards, mine, length) for a in (query_in, key_in, value_in, grad_out)], axis=1
+    )
+    arrived = lax.all_to_all(sent, "ctx", 0, 0, tiled=True)
+    at = device * mine
+    kern = lax.dynamic_slice_in_dim(short_kernel.reshape(9, channels), at, mine, 1)
+    fout = lax.dynamic_slice_in_dim(filter_out, at, mine, 1)
+    decay = lax.dynamic_slice_in_dim(filter_decay[None], at, mine, 1)
+    skip = lax.dynamic_slice_in_dim(skip_gain[None], at, mine, 1)
+    tokens = jax.ShapeDtypeStruct((RADIX, outer, LANES), F32)
+    hidden, slope, window, taps, spec = pl.pallas_call(
+        prepare_kernel,
+        out_shape=(
+            jax.ShapeDtypeStruct((order, sequence), F32),
+            jax.ShapeDtypeStruct((order, sequence), F32),
+            tokens,
+            tokens,
+            jax.ShapeDtypeStruct((RADIX, 2 * outer, LANES), F32),
+        ),
+        scratch_shapes=[pltpu.VMEM((RADIX, 2 * outer, LANES), F32)],
+        compiler_params=pltpu.CompilerParams(vmem_limit_bytes=40 << 20),
+        name="prepare",
+    )(filter_in, fout, decay, basis, twice, low)
+    results, grads, first = pl.pallas_call(
+        main_kernel,
+        out_shape=(
+            jax.ShapeDtypeStruct(arrived.shape, BF16),
+            jax.ShapeDtypeStruct((16 + order, LANES), F32),
+            jax.ShapeDtypeStruct((features, order), F32),
+        ),
+        scratch_shapes=[
+            pltpu.VMEM((4, RADIX, outer, LANES), F32),
+            pltpu.VMEM((RADIX, outer, LANES), F32),
+            pltpu.VMEM((RADIX, outer, LANES), F32),
+            pltpu.VMEM((3, RADIX, outer, LANES), F32),
+            pltpu.VMEM((RADIX, 2 * outer, 2 * LANES), F32),
+            pltpu.VMEM((RADIX, 2 * outer, 3 * LANES), BF16),
+            pltpu.VMEM((RADIX, 2 * outer, 3 * LANES), BF16),
+            pltpu.VMEM((3, RADIX, outer, LANES), F32),
+            pltpu.VMEM((sequence, LANES), F32),
+            pltpu.VMEM((4, RADIX, outer, LANES), BF16),
+        ],
+        compiler_params=pltpu.CompilerParams(vmem_limit_bytes=56 << 20),
+        name="main",
+    )(arrived, kern, skip, hidden, slope, window, taps, spec, fout, basis, twice, low, pair, turn)
+    returned = lax.all_to_all(results, "ctx", 0, 0, tiled=True)
+    total = first.reshape(-1, LANES)
+    by = 1
+    while by < groups:
+        total = total + exchange(total, "chan", by)
+        by *= 2
+    gathered = grads[None]
+    by = shards // 2
+    while by:
+        packed = jnp.concatenate([gathered.reshape(-1, LANES), total], axis=0)
+        other = exchange(packed, "ctx", by)
+        gathered = jnp.concatenate(
+            [gathered, other[: -total.shape[0]].reshape(gathered.shape)], axis=0
+        )
+        total = total + other[-total.shape[0] :]
+        by //= 2
+    place = jnp.zeros((shards,), jnp.int32)
+    index = jnp.arange(shards, dtype=jnp.int32) ^ device
+    by, weight = shards // 2, 1
+    while by:
+        place = place + jnp.where(index & by, weight, 0)
+        by, weight = by // 2, weight * 2
+    gathered = gathered[place].transpose(1, 0, 2).reshape(-1, channels)
+    outs = [returned[:, a].reshape(channels, length) for a in range(4)]
+    return (
+        *outs,
+        gathered[:9].reshape(3, 3, channels),
+        total.reshape(features, order),
+        gathered[16:],
+        gathered[9],
+        gathered[10],
+    )
+
+
+def body(*args):
+    channels, length = args[0].shape
+    shards = lax.axis_size("ctx")
+    whole = channels == shards * LANES and length == LANES and shards * length == RADIX * LANES
+    return blocks_body(*args) if whole else spread_body(*args)
+
+
 def solution(mesh):
     placed = (
         P("chan", "ctx"),

time: 659 us -> 87.6 us (0.13); the launches traced: 651 us -> 86.8 us
  waiting for transfers between devices: 240 us -> 39.2 us
  matrix products: 162 us -> 0 us
  blocking collectives: 78.2 us -> 0 us
  local copies, waits for them, and re-layouts: 82.3 us -> 13.4 us
  starting transfers between devices: 44.2 us -> 18 us
  other arithmetic: 27.9 us -> 2.45 us
  between operations: 15.5 us -> 0.83 us
  Pallas kernels: 0 us -> 13 us
    all_to_all x8 -> x2, waiting for transfers between devices: 216 us -> 15.7 us  [the longest x1 15.7 us: blocks_body(): arrived = lax.all_to_all(sent, 'ctx', 0, 0, tiled=True)]
    dot_general x45 -> x0, matrix products: 162 us -> none  [the longest x40 156 us: contract(): return jnp.einsum(form, left, right, precision=PRECISE)]
    psum x2 -> x0, blocking collectives: 78.2 us -> none  [the longest x1 40.9 us: body(): in_sum = lax.psum(in_terms, ('ctx', 'chan'))]
    all_to_all x8 -> x2, starting transfers between devices: 38 us -> 12.4 us  [the longest x1 7.4 us: blocks_body(): arrived = lax.all_to_all(sent, 'ctx', 0, 0, tiled=True)]
    another operation x7 -> x0, local copies, waits for them, and re-layouts: 22.5 us -> none  [the longest x2 8.18 us: inverse_columns(): jnp.stack([real_part, imag_part])]
    psum x1 -> x0, waiting for transfers between devices: 21.3 us -> none  [body(): lax.psum((short_terms, out_terms, decay_terms, skip_terms), 'ctx')]
    ppermute x2 -> x5, waiting for transfers between devices: 2.95 us -> 23.5 us  [exchange(): lax.ppermute(value, axis, [(i, i ^ by) for i in range(lax.axis_size(axis))])]
    slice x20 -> x7, local copies, waits for them, and re-layouts: 19.5 us -> 2.34 us  [the longest x1 0.98 us: blocks_body(): outs = [returned[:, a].reshape(channels, length) for a in range(4)]]
  transfers between devices with their start and end apart: 11 -> 7, of which waited for: 10 -> 5; matrix products, arithmetic and copies ran while one was open for 22% -> 7% of each run, Pallas kernels for 0% -> 3%
where the time goes in v1:
time: 87.6 us; the launch traced here: 86.8 us
  waiting for transfers between devices  39.2 us (45%)
  starting transfers between devices  18 us (21%)
  local copies, waits for them, and re-layouts  13.4 us (15%)
  Pallas kernels  13 us (15%)
  other arithmetic  2.45 us (3%)
    ppermute x5, waiting for transfers between devices, exchange(): lax.ppermute(value, axis, [(i, i ^ by) for i in range(lax.axis_size(axis))])  23.5 us
    all_to_all x1, waiting for transfers between devices, blocks_body(): arrived = lax.all_to_all(sent, 'ctx', 0, 0, tiled=True)  15.7 us
    pallas_call x1, Pallas kernels, blocks_body(): pl.pallas_call(main_kernel, out_shape=(jax.ShapeDtypeStruct(arrived.shape...  10.3 us
    all_to_all x1, starting transfers between devices, blocks_body(): arrived = lax.all_to_all(sent, 'ctx', 0, 0, tiled=True)  7.4 us
    unnamed x28, local copies, waits for them, and re-layouts  5.71 us
    ppermute x5, starting transfers between devices, exchange(): lax.ppermute(value, axis, [(i, i ^ by) for i in range(lax.axis_size(axis))])  5.53 us
    all_to_all x1, starting transfers between devices, blocks_body(): returned = lax.all_to_all(results, 'ctx', 0, 0, tiled=True)  5.04 us
    pallas_call x1, Pallas kernels, blocks_body(): pl.pallas_call(prepare_kernel, out_shape=(jax.ShapeDtypeStruct((order, se...  2.63 us
  transfers between devices with their start and end apart: 7, of which 5 were waited for; matrix products, arithmetic and copies ran while one was open for 7% of the time, Pallas kernels for 3%

profile of v1, /device:TPU:0, one launch (start us, length us, event | category | flops | bytes accessed | tf_op | source)
XLA Modules:
  0.0 86.8 jit_solution(1439252964604519435)
XLA Ops:
  0.6 0.0 copy-start
  0.7 2.3 %pad_maximum_fusion = bf16[8,4,128,128]{3,2,1,0:T(8,128)(2,1)} fusion(bf16[8,1,128,128]{3,2,1,0:T(8,128)(2,1)} %bitcast.40, bf16[8,1,128,128]{3,2,1,0:T(8,128)(2,1)} %bitcast.41, bf16[8,1,128,128]{3,2,1,0:T(8,128)(2,1)} %bitcast.42, bf16[8,1,128,128]{3,2,1,0:T(8,128)(2,1)} %bitcast.43), kind=kLoop, calls=%fused_computation.1 | loop fusion | flops 1572864 | bytes 2097152 | tf_op jit(solution)/shard_map/stack | solution.py:542
  3.0 0.0 copy-start.13
  3.0 0.0 copy-start.1
  3.0 0.0 copy-start.2
  3.0 0.0 copy-start.4
  3.0 7.4 %all-to-all-start = ((bf16[8,4,128,128]{3,2,1,0:T(8,128)(2,1)}), bf16[8,4,128,128]{3,2,1,0:T(8,128)(2,1)S(1)}, u32[]{:S(2)}, u32[]{:S(2)}) async-start(bf16[8,4,128,128]{3,2,1,0:T(8,128)(2,1)} %pad_maximum_fusion), calls=%async_computation | async-start | bytes 2097152 | tf_op jit(solution)/shard_map/all_to_all | solution.py:545
  10.4 0.0 copy-done.13
  10.4 0.8 dynamic-slice_bitcast_fusion.decay_ref
  11.2 0.0 copy-done
  11.2 0.0 copy-start.10
  11.2 0.0 copy-done.1
  11.2 0.0 copy-done.2
  11.2 0.0 copy-done.4
  11.2 0.7 copy-done.10
  12.0 0.0 copy-start.7
  12.0 2.6 %prepare.1 = (f32[64,1024]{1,0:T(8,128)S(1)}, f32[64,1024]{1,0:T(8,128)S(1)}, f32[8,128,128]{2,1,0:T(8,128)S(1)}, f32[8,128,128]{2,1,0:T(8,128)S(1)}, f32[8,256,128]{2,1,0:T(8,128)S(1)}) custom-call(f32[64,64]{1,0:T(8,128)S(1)} %copy-done.10, f32[64,128]{1,0:T(8,128)S(1)} %constant_dynamic-slice_fusion.fout_ref, ...), custom_call_target="tpu_custom_call" | custom-call | tf_op jit(solution)/shard_map/prepare/pallas_call | solution.py:552
  14.6 0.0 copy-done.7
  14.6 0.0 copy-start.3
  14.6 1.0 %copy-done.3 = f32[8,256,128]{2,1,0:T(8,128)} copy-done((f32[8,256,128]{2,1,0:T(8,128)}, f32[8,256,128]{2,1,0:T(8,128)S(1)}, u32[]{:S(2)}) %copy-start.3) | copy-done | bytes 1048600
  15.6 0.0 copy-start.5
  15.6 0.8 copy-done.5
  16.4 0.0 copy-start.6
  16.4 0.8 copy-done.6
  17.2 0.0 copy-start.8
  17.2 0.7 copy-done.8
  17.9 0.0 copy-start.9
  17.9 0.7 copy-done.9
  18.6 1.3 %dynamic-slice_bitcast_fusion.1.skip_ref = f32[1,128]{1,0:T(1,128)} fusion(f32[1024]{0:T(1024)} %param.21, s32[]{:T(128)S(6)} %select_n.47), kind=kLoop, calls=%fused_computation.23 | loop fusion | bytes 1028 | tf_op jit(solution)/shard_map/dynamic_slice | solution.py:550
  19.9 0.6 constant_dynamic-slice_fusion.1.kern_ref
  20.5 15.7 %all-to-all-done.in_ref = bf16[8,4,128,128]{3,2,1,0:T(8,128)(2,1)S(1)} async-done(((bf16[8,4,128,128]{3,2,1,0:T(8,128)(2,1)}), bf16[8,4,128,128]{3,2,1,0:T(8,128)(2,1)S(1)}, u32[]{:S(2)}, u32[]{:S(2)}) %all-to-all-start) | async-done | bytes 1048608 | tf_op jit(solution)/shard_map/all_to_all | solution.py:545
  36.2 0.0 copy-start.11
  36.2 1.0 %copy-done.11 = bf16[8,4,128,128]{3,2,1,0:T(8,128)(2,1)} copy-done((bf16[8,4,128,128]{3,2,1,0:T(8,128)(2,1)}, bf16[8,4,128,128]{3,2,1,0:T(8,128)(2,1)S(1)}, u32[]{:S(2)}) %copy-start.11) | copy-done | bytes 1048600
  37.1 10.3 %main.1 = (bf16[8,4,128,128]{3,2,1,0:T(8,128)(2,1)}, f32[80,128]{1,0:T(8,128)}, f32[64,64]{1,0:T(8,128)}) custom-call(bf16[8,4,128,128]{3,2,1,0:T(8,128)(2,1)} %copy-done.11, f32[9,128]{1,0:T(8,128)} %constant_dynamic-slice_fusion.1.kern_ref, f32[1,128]{1,0:T(1,128)} %dynamic-slice_bitcast_fusion.1.skip_ref, f32[64,1024]{1,0:T(8,128)} %copy-done.8, ...), custom_call_target="tpu_custom_call" | custom-call | tf_op jit(solution)/shard_map/main/pallas_call | solution.py:565
  47.5 0.8 reshape.105
  48.3 0.0 copy-start.12
  48.3 0.0 collective-permute-start
  48.3 1.2 %collective-permute-done = f32[32,128]{1,0:T(8,128)S(1)} collective-permute-done((f32[32,128]{1,0:T(8,128)S(1)}, f32[32,128]{1,0:T(8,128)S(1)}, u32[]{:S(2)}, u32[]{:S(2)}) %collective-permute-start) | collective-permute-done | bytes 16416 | tf_op jit(solution)/shard_map/ppermute | solution.py:526
  49.5 1.5 %collective-permute-start.1 = (f32[32,128]{1,0:T(8,128)S(1)}, f32[32,128]{1,0:T(8,128)S(1)}, u32[]{:S(2)}, u32[]{:S(2)}) collective-permute-start(f32[32,128]{1,0:T(8,128)S(1)} %add.52), channel_id=1, source_target_pairs={{0,2},{1,3},{2,0},{3,1},{4,6},{5,7},{6,4},{7,5},{8,10},{9,11},{10,... | collective-permute-start | bytes 49160 | tf_op jit(solution)/shard_map/ppermute | solution.py:526
  51.0 2.2 %collective-permute-done.1 = f32[32,128]{1,0:T(8,128)S(1)} collective-permute-done((f32[32,128]{1,0:T(8,128)S(1)}, f32[32,128]{1,0:T(8,128)S(1)}, u32[]{:S(2)}, u32[]{:S(2)}) %collective-permute-start.1) | collective-permute-done | bytes 16416 | tf_op jit(solution)/shard_map/ppermute | solution.py:526
  53.2 0.0 copy-done.12
  53.2 0.1 collective-permute-start.2
  53.3 5.0 %all-to-all-start.1 = ((bf16[8,4,128,128]{3,2,1,0:T(8,128)(2,1)}), bf16[8,4,128,128]{3,2,1,0:T(8,128)(2,1)S(1)}, u32[]{:S(2)}, u32[]{:S(2)}) async-start(bf16[8,4,128,128]{3,2,1,0:T(8,128)(2,1)} %get-tuple-element.22), calls=%async_computation.1 | async-start | bytes 2097152 | tf_op jit(solution)/shard_map/all_to_all | solution.py:587
  58.4 0.0 collective-permute-done.2
  58.4 2.1 %collective-permute-start.3 = (f32[192,128]{1,0:T(8,128)S(1)}, f32[192,128]{1,0:T(8,128)S(1)}, u32[]{:S(2)}, u32[]{:S(2)}) collective-permute-start(f32[192,128]{1,0:T(8,128)S(1)} %pad_maximum_fusion.4), channel_id=1, source_target_pairs={{0,8},{4,12},{8,0},{12,4},{16,24},{20,28},{24,16},{28,20},{1,9},{5... | collective-permute-start | bytes 294920 | tf_op jit(solution)/shard_map/ppermute | solution.py:526
  60.5 16.0 %collective-permute-done.3 = f32[192,128]{1,0:T(8,128)S(1)} collective-permute-done((f32[192,128]{1,0:T(8,128)S(1)}, f32[192,128]{1,0:T(8,128)S(1)}, u32[]{:S(2)}, u32[]{:S(2)}) %collective-permute-start.3) | collective-permute-done | bytes 98336 | tf_op jit(solution)/shard_map/ppermute | solution.py:526
  76.5 1.9 %collective-permute-start.4 = (f32[352,128]{1,0:T(8,128)S(1)}, f32[352,128]{1,0:T(8,128)S(1)}, u32[]{:S(2)}, u32[]{:S(2)}) collective-permute-start(f32[352,128]{1,0:T(8,128)S(1)} %pad_maximum_fusion.2), channel_id=1, source_target_pairs={{0,4},{4,0},{8,12},{12,8},{16,20},{20,16},{24,28},{28,24},{1,5},{5... | collective-permute-start | bytes 540680 | tf_op jit(solution)/shard_map/ppermute | solution.py:526
  78.4 4.1 %collective-permute-done.4 = f32[352,128]{1,0:T(8,128)S(1)} collective-permute-done((f32[352,128]{1,0:T(8,128)S(1)}, f32[352,128]{1,0:T(8,128)S(1)}, u32[]{:S(2)}, u32[]{:S(2)}) %collective-permute-start.4) | collective-permute-done | bytes 180256 | tf_op jit(solution)/shard_map/ppermute | solution.py:526
  82.5 0.7 reshape.112
  83.3 0.6 gather_fusion
  83.9 0.6 reshape.111
  84.5 0.6 fusion.4
  85.1 0.7 copy_bitcast_fusion
  85.8 0.0 all-to-all-done.1
  85.8 1.0 %fusion.3 = (bf16[8,1,128,128]{3,2,1,0:T(8,128)(2,1)}, bf16[8,1,128,128]{3,2,1,0:T(8,128)(2,1)}, bf16[8,1,128,128]{3,2,1,0:T(8,128)(2,1)}, bf16[8,1,128,128]{3,2,1,0:T(8,128)(2,1)}) fusion(bf16[8,4,128,128]{3,2,1,0:T(8,128)(2,1)S(1)} %all-to-all-done.1), kind=kLoop, calls=%fused_computation.26 | loop fusion | bytes 2097152 | tf_op jit(solution)/shard_map/slice | solution.py:610
  (20 shorter events, 0.2 us)
Async XLA Ops:
  0.6 10.6 %copy-start = (f32[64,1024]{1,0:T(8,128)S(1)}, f32[64,1024]{1,0:T(8,128)}, u32[]{:S(2)}) copy-start(f32[64,1024]{1,0:T(8,128)} %param.19) | copy-start | bytes 786436
  3.0 7.4 %copy-start.13 = (f32[3,3,1024]{2,1,0:T(4,128)S(1)}, f32[3,3,1024]{2,1,0:T(4,128)}, u32[]{:S(2)}) copy-start(f32[3,3,1024]{2,1,0:T(4,128)} %param.17) | copy-start | bytes 110596
  3.0 8.2 %copy-start.1 = (bf16[8,256,256]{2,1,0:T(8,128)(2,1)S(1)}, bf16[8,256,256]{2,1,0:T(8,128)(2,1)}, u32[]{:S(2)}) copy-start(bf16[8,256,256]{2,1,0:T(8,128)(2,1)} %constant.38.clone.twice_ref) | copy-start | bytes 3145732
  3.0 8.2 %copy-start.2 = (bf16[8,256,128]{2,1,0:T(8,128)(2,1)S(1)}, bf16[8,256,128]{2,1,0:T(8,128)(2,1)}, u32[]{:S(2)}) copy-start(bf16[8,256,128]{2,1,0:T(8,128)(2,1)} %constant.39.clone.low_ref) | copy-start | bytes 1572868
  3.0 8.2 %copy-start.4 = (f32[64,1024]{1,0:T(8,128)S(1)}, f32[64,1024]{1,0:T(8,128)}, u32[]{:S(2)}) copy-start(f32[64,1024]{1,0:T(8,128)} %constant.41.clone.basis_ref) | copy-start | bytes 786436
  3.0 33.2 %all-to-all-start = ((bf16[8,4,128,128]{3,2,1,0:T(8,128)(2,1)}), bf16[8,4,128,128]{3,2,1,0:T(8,128)(2,1)S(1)}, u32[]{:S(2)}, u32[]{:S(2)}) async-start(bf16[8,4,128,128]{3,2,1,0:T(8,128)(2,1)} %pad_maximum_fusion), calls=%async_computation | async-start | bytes 2097152 | tf_op jit(solution)/shard_map/all_to_all | solution.py:545
  11.2 0.8 copy-start.10
  12.0 2.6 %copy-start.7 = (f32[64,128]{1,0:T(8,128)}, f32[64,128]{1,0:T(8,128)S(1)}, u32[]{:S(2)}) copy-start(f32[64,128]{1,0:T(8,128)S(1)} %constant_dynamic-slice_fusion.fout_ref) | copy-start | bytes 98308
  14.6 1.0 %copy-start.3 = (f32[8,256,128]{2,1,0:T(8,128)}, f32[8,256,128]{2,1,0:T(8,128)S(1)}, u32[]{:S(2)}) copy-start(f32[8,256,128]{2,1,0:T(8,128)S(1)} %get-tuple-element.21.spec_ref) | copy-start | bytes 3145732
  15.6 0.8 copy-start.5
  16.4 0.8 copy-start.6
  17.2 0.7 copy-start.8
  17.9 0.7 copy-start.9
  36.2 1.0 %copy-start.11 = (bf16[8,4,128,128]{3,2,1,0:T(8,128)(2,1)}, bf16[8,4,128,128]{3,2,1,0:T(8,128)(2,1)S(1)}, u32[]{:S(2)}) copy-start(bf16[8,4,128,128]{3,2,1,0:T(8,128)(2,1)S(1)} %all-to-all-done.in_ref) | copy-start | bytes 3145732
  48.3 4.9 %copy-start.12 = (f32[80,128]{1,0:T(8,128)S(1)}, f32[80,128]{1,0:T(8,128)}, u32[]{:S(2)}) copy-start(f32[80,128]{1,0:T(8,128)} %get-tuple-element.23) | copy-start | bytes 122884
  48.3 1.2 %collective-permute-start = (f32[32,128]{1,0:T(8,128)S(1)}, f32[32,128]{1,0:T(8,128)S(1)}, u32[]{:S(2)}, u32[]{:S(2)}) collective-permute-start(f32[32,128]{1,0:T(8,128)S(1)} %reshape.105), channel_id=1, source_target_pairs={{0,1},{1,0},{2,3},{3,2},{4,5},{5,4},{6,7},{7,6},{8,9},{9,8},{10,11... | collective-permute-start | bytes 49160 | tf_op jit(solution)/shard_map/ppermute | solution.py:526
  49.5 3.7 %collective-permute-start.1 = (f32[32,128]{1,0:T(8,128)S(1)}, f32[32,128]{1,0:T(8,128)S(1)}, u32[]{:S(2)}, u32[]{:S(2)}) collective-permute-start(f32[32,128]{1,0:T(8,128)S(1)} %add.52), channel_id=1, source_target_pairs={{0,2},{1,3},{2,0},{3,1},{4,6},{5,7},{6,4},{7,5},{8,10},{9,11},{10,... | collective-permute-start | bytes 49160 | tf_op jit(solution)/shard_map/ppermute | solution.py:526
  53.2 5.1 %collective-permute-start.2 = (f32[112,128]{1,0:T(8,128)S(1)}, f32[112,128]{1,0:T(8,128)S(1)}, u32[]{:S(2)}, u32[]{:S(2)}) collective-permute-start(f32[112,128]{1,0:T(8,128)S(1)} %pad_maximum_fusion.6), channel_id=1, source_target_pairs={{0,16},{4,20},{8,24},{12,28},{16,0},{20,4},{24,8},{28,12},{1,17},{... | collective-permute-start | bytes 172040 | tf_op jit(solution)/shard_map/ppermute | solution.py:526
  53.3 32.5 %all-to-all-start.1 = ((bf16[8,4,128,128]{3,2,1,0:T(8,128)(2,1)}), bf16[8,4,128,128]{3,2,1,0:T(8,128)(2,1)S(1)}, u32[]{:S(2)}, u32[]{:S(2)}) async-start(bf16[8,4,128,128]{3,2,1,0:T(8,128)(2,1)} %get-tuple-element.22), calls=%async_computation.1 | async-start | bytes 2097152 | tf_op jit(solution)/shard_map/all_to_all | solution.py:587
  58.4 18.0 %collective-permute-start.3 = (f32[192,128]{1,0:T(8,128)S(1)}, f32[192,128]{1,0:T(8,128)S(1)}, u32[]{:S(2)}, u32[]{:S(2)}) collective-permute-start(f32[192,128]{1,0:T(8,128)S(1)} %pad_maximum_fusion.4), channel_id=1, source_target_pairs={{0,8},{4,12},{8,0},{12,4},{16,24},{20,28},{24,16},{28,20},{1,9},{5... | collective-permute-start | bytes 294920 | tf_op jit(solution)/shard_map/ppermute | solution.py:526
  76.5 6.0 %collective-permute-start.4 = (f32[352,128]{1,0:T(8,128)S(1)}, f32[352,128]{1,0:T(8,128)S(1)}, u32[]{:S(2)}, u32[]{:S(2)}) collective-permute-start(f32[352,128]{1,0:T(8,128)S(1)} %pad_maximum_fusion.2), channel_id=1, source_target_pairs={{0,4},{4,0},{8,12},{12,8},{16,20},{20,16},{24,28},{28,24},{1,5},{5... | collective-permute-start | bytes 540680 | tf_op jit(solution)/shard_map/ppermute | solution.py:526
